TPU v7x, 128 devices: a whole 4x4x4 slice. The times are simulated.
128 devices in a mesh: row: 16 (over y, x), col: 4 (over z), dp: 2 (over core).
Axes of the slice: x: 4, y: 4, z: 4, core: 2. Of those that a mesh axis runs over, the one named last changes fastest.
Arguments:
- inputs: bfloat16 [1024, 8192], P(('col', 'dp'), 'row'), may hold values from -6 to 6
- gate_weight: bfloat16 [8192, 14336], P('row', 'col'), may hold values from -0.0625 to 0.0625
- up_weight: bfloat16 [8192, 14336], P('row', 'col'), may hold values from -0.0625 to 0.0625
- down_weight: bfloat16 [14336, 8192], P('col', 'row'), may hold values from -0.046875 to 0.046875
- reward_head: bfloat16 [8192], P('row'), may hold values from -0.0625 to 0.0625
- upstream: bfloat16 [1024, 8192], P(('col', 'dp'), 'row'), may hold values from -0.59765625 to 0.59765625
- labels: int32 [1024], P(('col', 'dp')), may hold values from 0 to 1
- label_mask: int32 [1024], P(('col', 'dp')), may hold values 0 or 1
Outputs:
- gate_grad: float32 [8192, 14336], P(('row', 'dp'), 'col')
- up_grad: float32 [8192, 14336], P(('row', 'dp'), 'col')
- down_grad: float32 [14336, 8192], P(('col', 'dp'), 'row')
- input_grad: float32 [1024, 8192], P(('col', 'dp'), 'row')
All inputs are finite; a program needn't handle non-finite values. No bound on the sum of `label_mask` on one device may be relied on, other than what follows from the above.
Results may differ from a plain program's by a relative error of at most 0.035.
Values may be sent and summed in bfloat16 or wider, within the bound.
No kernel may reach another device: no remote copies, remote signals or barrier semaphores. Data moves between devices by JAX's collectives and lax.ppermute only.
A program may use at most 128 MiB of HBM per device.

v0:
```python
import jax
import jax.numpy as jnp
from jax import lax
from jax.sharding import PartitionSpec as P

reward_weight = 8.0


def transpose_product(left, right):
    return lax.dot_general(
        left, right, (((0,), (0,)), ((), ())), preferred_element_type=jnp.float32
    )


def right_transpose(left, right):
    return lax.dot_general(
        left, right, (((1,), (1,)), ((), ())), preferred_element_type=jnp.float32
    )


def gather_tokens(block):
    return lax.all_gather(block, "col", axis=0, tiled=True)


def gather_hidden(stacked):
    return lax.all_gather(stacked, "row", axis=1, tiled=True)


def column_total(term_fn, count_rows):
    return lax.psum_scatter(
        term_fn(jnp.int32(0), count_rows * lax.axis_size("col")).astype(jnp.bfloat16),
        "col",
        scatter_dimension=0,
        tiled=True,
    ).astype(jnp.float32)


def per_device(
    inputs, gate_weight, up_weight, down_weight, reward_head, upstream, labels, label_mask
):
    width = gate_weight.shape[1]
    gathered = gather_tokens(inputs)
    rows = gathered
    joined = lax.psum_scatter(
        jnp.concatenate(
            [
                jnp.dot(rows, gate_weight, preferred_element_type=jnp.float32),
                jnp.dot(rows, up_weight, preferred_element_type=jnp.float32),
            ],
            axis=1,
        ).astype(jnp.bfloat16),
        "row",
        scatter_dimension=0,
        tiled=True,
    ).astype(jnp.float32)
    gate = joined[:, :width]
    upper = joined[:, width:]
    sigmoid_gate = jax.nn.sigmoid(gate)
    hidden = (gate * sigmoid_gate * upper).astype(jnp.bfloat16)
    hidden_all = gather_hidden(hidden[None])[0]

    def output_term(start, count):
        return jnp.dot(hidden_all, down_weight, preferred_element_type=jnp.float32)

    mixed = column_total(output_term, inputs.shape[0])
    outcome = inputs.astype(jnp.float32) + mixed
    head_value = reward_head.astype(jnp.float32)
    partial_score = jnp.dot(outcome, head_value, precision=lax.Precision.HIGHEST)
    score = lax.psum(partial_score, "row")
    slope = (
        reward_weight
        * label_mask.astype(jnp.float32)
        * (jax.nn.sigmoid(score) - labels.astype(jnp.float32))
    )
    grad_out = upstream.astype(jnp.float32) + slope[:, None] * head_value[None, :]
    grad_mixed = grad_out.astype(jnp.bfloat16)
    grad_rows = gather_tokens(grad_mixed)
    rows = grad_rows
    grad_hidden = lax.psum_scatter(
        right_transpose(rows, down_weight).astype(jnp.bfloat16),
        "row",
        scatter_dimension=0,
        tiled=True,
    ).astype(jnp.float32)
    grad_gate = (grad_hidden * upper * sigmoid_gate * (1.0 + gate * (1.0 - sigmoid_gate))).astype(
        jnp.bfloat16
    )
    grad_upper = (grad_hidden * gate * sigmoid_gate).astype(jnp.bfloat16)
    grads_all = gather_hidden(jnp.stack([grad_gate, grad_upper]))

    def input_term(start, count):
        return right_transpose(grads_all[0], gate_weight) + right_transpose(grads_all[1], up_weight)

    input_grad = grad_out + column_total(input_term, inputs.shape[0])
    gate_grad, up_grad, down_grad = (
        lax.psum_scatter(
            transpose_product(gathered, grads_all[0]).astype(jnp.bfloat16),
            "dp",
            scatter_dimension=0,
            tiled=True,
        ).astype(jnp.float32),
        lax.psum_scatter(
            transpose_product(gathered, grads_all[1]).astype(jnp.bfloat16),
            "dp",
            scatter_dimension=0,
            tiled=True,
        ).astype(jnp.float32),
        lax.psum_scatter(
            transpose_product(hidden_all, grad_rows).astype(jnp.bfloat16),
            "dp",
            scatter_dimension=0,
            tiled=True,
        ).astype(jnp.float32),
    )
    return (gate_grad, up_grad, down_grad, input_grad)


def solution(mesh):
    in_specs = (
        P(("col", "dp"), "row"),
        P("row", "col"),
        P("row", "col"),
        P("col", "row"),
        P("row"),
        P(("col", "dp"), "row"),
        P(("col", "dp")),
        P(("col", "dp")),
    )
    out_specs = (
        P(("row", "dp"), "col"),
        P(("row", "dp"), "col"),
        P(("col", "dp"), "row"),
        P(("col", "dp"), "row"),
    )
    return jax.shard_map(
        per_device, mesh=mesh, in_specs=in_specs, out_specs=out_specs, check_vma=False
    )
```

profile of v0, /device:TPU:1, one launch (start us, length us, event | category | flops | bytes accessed | tf_op | source)
XLA Modules:
  0.0 488.5 jit_solution(17730826505208931112)
XLA Ops:
  7.2 0.0 reduce-scatter.8.cloned.1.call-start
  7.2 13.6 %all_gather.12 = bf16[512,512]{1,0:T(8,128)(2,1)S(1)} all-gather(bf16[128,512]{1,0:T(8,128)(2,1)} %param.8), channel_id=1, replica_groups=mesh['row'=16,'col'=4,'dp'=2] {'col'}, dimensions={0}, use_global_device_ids=true | all-gather | bytes 655360 | tf_op jit(solution)/shard_map/all_gather | solution.py:22
  20.8 0.0 copy-start.6
  20.8 4.3 convolution_convert_fusion.4
  25.1 0.0 copy-done.6
  25.1 3.9 convolution_convert_fusion.5
  29.0 6.0 %pad_maximum_fusion = bf16[512,7168]{1,0:T(8,128)(2,1)} fusion(bf16[512,3584]{1,0:T(8,128)(2,1)S(1)} %convolution_convert_fusion.4, bf16[512,3584]{1,0:T(8,128)(2,1)} %convolution_convert_fusion.5), kind=kLoop, calls=%fused_computation | loop fusion | flops 14680064 | bytes 14680064 | tf_op jit(solution)/shard_map/concatenate | solution.py:45
  35.0 0.0 reduce-scatter.8.cloned.1.call-update
  35.0 0.0 all-gather.6.cloned.1.call-start
  35.1 84.9 %reduce-scatter.8.cloned.1.call-done = bf16[32,7168]{1,0:T(8,128)(2,1)} async-done(((bf16[512,7168]{1,0:T(8,128)(2,1)}), bf16[32,7168]{1,0:T(8,128)(2,1)}) %reduce-scatter.8.cloned.1.call-update) | async-done | bytes 458768 | tf_op jit(solution)/shard_map/reduce_scatter | solution.py:44
  120.0 1.1 convert_element_type.76
  121.1 0.8 multiply_convert_fusion
  121.9 0.0 all-gather.6.cloned.1.call-update
  121.9 0.0 copy-start.2
  121.9 0.0 copy-start
  122.0 0.0 copy-start.3
  122.0 0.0 copy-start.4
  122.0 0.0 copy-start.1
  122.0 0.0 reduce-scatter.10.cloned.1.call-start
  122.0 50.6 %all-gather.6.cloned.1.call-done = bf16[512,3584]{1,0:T(8,128)(2,1)} async-done(((bf16[32,3584]{1,0:T(8,128)(2,1)}), bf16[512,3584]{1,0:T(8,128)(2,1)}) %all-gather.6.cloned.1.call-update) | async-done | bytes 3670032 | tf_op jit(solution)/shard_map/all_gather | solution.py:26
  172.7 6.0 %convolution_convert_fusion.6 = bf16[512,512]{1,0:T(8,128)(2,1)} fusion(bf16[512,3584]{1,0:T(8,128)(2,1)} %all-gather.6.cloned.1.call-done, bf16[3584,512]{1,0:T(8,128)(2,1)} %param.11), kind=kOutput, calls=%fused_computation.15 | convolution fusion | flops 1879310336 | bytes 7864320 | tf_op jit(solution)/shard_map/dot_general | solution.py:63
  178.7 0.0 reduce-scatter.10.cloned.1.call-update
  178.7 0.0 reduce-scatter.12.cloned.1.call-start
  178.7 0.0 copy-done.2
  178.8 19.6 %reduce-scatter.10.cloned.1.call-done = bf16[128,512]{1,0:T(8,128)(2,1)} async-done(((bf16[512,512]{1,0:T(8,128)(2,1)}), bf16[128,512]{1,0:T(8,128)(2,1)}) %reduce-scatter.10.cloned.1.call-update) | async-done | bytes 131088 | tf_op jit(solution)/shard_map/reduce_scatter | solution.py:30
  198.4 0.0 copy-done
  198.4 1.1 convolution_bitcast_fusion
  199.5 33.2 %psum.7 = f32[128]{0:T(128)S(1)} all-reduce(f32[128]{0:T(128)S(1)} %convolution_bitcast_fusion), channel_id=1, replica_groups=mesh['row'=16,'col'=4,'dp'=2] {'row'}, use_global_device_ids=true, to_apply=%region_2.0 | all-reduce | flops 128 | bytes 1024 | tf_op jit(solution)/shard_map/psum | solution.py:69
  232.7 0.0 copy-done.3
  232.7 0.0 copy-done.4
  232.7 0.0 copy-done.1
  232.7 0.1 fusion.14
  232.8 10.2 %all_gather.14 = bf16[512,512]{1,0:T(8,128)(2,1)S(1)} all-gather(bf16[128,512]{1,0:T(8,128)(2,1)S(1)} %fusion.14), channel_id=1, replica_groups=mesh['row'=16,'col'=4,'dp'=2] {'col'}, dimensions={0}, use_global_device_ids=true | all-gather | bytes 655360 | tf_op jit(solution)/shard_map/all_gather | solution.py:22
  243.0 6.0 %convolution_convert_fusion.3 = bf16[512,3584]{1,0:T(8,128)(2,1)} fusion(bf16[512,512]{1,0:T(8,128)(2,1)S(1)} %all_gather.14, bf16[3584,512]{1,0:T(8,128)(2,1)} %param.11), kind=kOutput, calls=%fused_computation.4 | convolution fusion | flops 1880883200 | bytes 7864320 | tf_op jit(solution)/shard_map/dot_general | solution.py:16
  249.0 0.0 reduce-scatter.12.cloned.1.call-update
  249.0 0.0 all-gather.4.cloned.1.call-start
  249.1 81.0 %reduce-scatter.12.cloned.1.call-done = bf16[32,3584]{1,0:T(8,128)(2,1)} async-done(((bf16[512,3584]{1,0:T(8,128)(2,1)}), bf16[32,3584]{1,0:T(8,128)(2,1)}) %reduce-scatter.12.cloned.1.call-update) | async-done | bytes 229392 | tf_op jit(solution)/shard_map/reduce_scatter | solution.py:79
  330.0 1.2 fusion.16
  331.2 0.8 pad_maximum_fusion.1
  332.0 0.0 all-gather.4.cloned.1.call-update
  332.0 0.0 reduce-scatter.18.cloned.1.call-start
  332.1 6.0 %convolution_convert_fusion = bf16[3584,512]{1,0:T(8,128)(2,1)} fusion(bf16[512,3584]{1,0:T(8,128)(2,1)} %all-gather.6.cloned.1.call-done, bf16[512,512]{1,0:T(8,128)(2,1)S(1)} %all_gather.14), kind=kOutput, calls=%fused_computation.1 | convolution fusion | flops 1880883200 | bytes 7864320 | tf_op jit(solution)/shard_map/dot_general | solution.py:10
  338.0 0.0 reduce-scatter.18.cloned.1.call-update
  338.1 0.0 reduce-scatter.20.cloned.1.call-start
  338.1 61.8 %all-gather.4.cloned.1.call-done = bf16[2,512,3584]{2,1,0:T(8,128)(2,1)} async-done(((bf16[2,32,3584]{2,1,0:T(8,128)(2,1)}), bf16[2,512,3584]{2,1,0:T(8,128)(2,1)}) %all-gather.4.cloned.1.call-update) | async-done | bytes 7340048 | tf_op jit(solution)/shard_map/all_gather | solution.py:26
  399.9 5.4 %fusion.2 = f32[512,512]{1,0:T(8,128)S(1)} fusion(bf16[512,3584]{1,0:T(8,128)(2,1)} %param.9, bf16[2,512,3584]{2,1,0:T(8,128)(2,1)} %all-gather.4.cloned.1.call-done), kind=kOutput, calls=%fused_computation.11 | convolution fusion | flops 1879048192 | bytes 8388608 | tf_op jit(solution)/shard_map/dot_general | solution.py:16
  405.3 0.0 copy-done.5
  405.3 0.9 copy-done.7
  406.1 2.9 fusion.5
  409.0 0.0 reduce-scatter.20.cloned.1.call-update
  409.1 0.2 reduce-scatter.16.cloned.1.call-start
  409.3 6.0 %fusion.1 = bf16[512,3584]{0,1:T(8,128)(2,1)} fusion(bf16[512,512]{1,0:T(8,128)(2,1)S(1)} %all_gather.12, bf16[2,512,3584]{2,1,0:T(8,128)(2,1)} %all-gather.4.cloned.1.call-done), kind=kOutput, calls=%fused_computation.8 | convolution fusion | flops 1880883200 | bytes 7864320 | tf_op jit(solution)/shard_map/dot_general | solution.py:10
  415.3 0.0 reduce-scatter.16.cloned.1.call-update
  415.3 0.0 reduce-scatter.14.cloned.1.call-start
  415.4 6.3 %fusion = bf16[512,3584]{0,1:T(8,128)(2,1)} fusion(bf16[512,512]{1,0:T(8,128)(2,1)S(1)} %all_gather.12, bf16[2,512,3584]{2,1,0:T(8,128)(2,1)} %all-gather.4.cloned.1.call-done), kind=kOutput, calls=%fused_computation.7 | convolution fusion | flops 1880883200 | bytes 7864320 | tf_op jit(solution)/shard_map/dot_general | solution.py:10
  421.6 0.0 reduce-scatter.14.cloned.1.call-update
  421.6 0.0 reduce-scatter.18.cloned.1.call-done
  421.7 3.9 convert_element_type.94
  425.5 14.9 %reduce-scatter.20.cloned.1.call-done = bf16[128,512]{1,0:T(8,128)(2,1)} async-done(((bf16[512,512]{1,0:T(8,128)(2,1)}), bf16[128,512]{1,0:T(8,128)(2,1)}) %reduce-scatter.20.cloned.1.call-update) | async-done | bytes 131088 | tf_op jit(solution)/shard_map/reduce_scatter | solution.py:30
  440.5 1.7 convert_add_fusion
  442.2 17.1 %reduce-scatter.16.cloned.1.call-done = bf16[256,3584]{0,1:T(8,128)(2,1)} async-done(((bf16[512,3584]{0,1:T(8,128)(2,1)}), bf16[256,3584]{0,1:T(8,128)(2,1)}) %reduce-scatter.16.cloned.1.call-update) | async-done | bytes 1835024 | tf_op jit(solution)/shard_map/reduce_scatter | solution.py:102
  459.3 4.0 copy.13
  463.3 14.7 %reduce-scatter.14.cloned.1.call-done = bf16[256,3584]{0,1:T(8,128)(2,1)} async-done(((bf16[512,3584]{0,1:T(8,128)(2,1)}), bf16[256,3584]{0,1:T(8,128)(2,1)}) %reduce-scatter.14.cloned.1.call-update) | async-done | bytes 1835024 | tf_op jit(solution)/shard_map/reduce_scatter | solution.py:96
  478.0 4.0 copy.12
  (5 shorter events, 0.0 us)
Async XLA Ops:
  7.2 112.8 %reduce-scatter.8.cloned.1.call-start = ((), (), s32[]{:S(2)}) async-start(), calls=%async_computation.7 | async-start | bytes 7798784 | tf_op jit(solution)/shard_map/reduce_scatter | solution.py:44
  20.8 4.3 copy-start.6
  35.0 137.6 %all-gather.6.cloned.1.call-start = ((), (), s32[]{:S(2)}) async-start(), calls=%async_computation.15 | async-start | bytes 3899392 | tf_op jit(solution)/shard_map/all_gather | solution.py:26
  121.9 56.8 %copy-start.2 = (bf16[512]{0:T(512)(128)(2,1)S(1)}, bf16[512]{0:T(512)(128)(2,1)}, u32[]{:S(2)}) copy-start(bf16[512]{0:T(512)(128)(2,1)} %param.12) | copy-start | bytes 3076
  121.9 76.5 %copy-start = (bf16[128,512]{1,0:T(8,128)(2,1)S(1)}, bf16[128,512]{1,0:T(8,128)(2,1)}, u32[]{:S(2)}) copy-start(bf16[128,512]{1,0:T(8,128)(2,1)} %param.8) | copy-start | bytes 393220
  122.0 110.7 %copy-start.3 = (s32[128]{0:T(128)S(1)}, s32[128]{0:T(128)}, u32[]{:S(2)}) copy-start(s32[128]{0:T(128)} %param.14) | copy-start | bytes 1540
  122.0 110.7 %copy-start.4 = (s32[128]{0:T(128)S(1)}, s32[128]{0:T(128)}, u32[]{:S(2)}) copy-start(s32[128]{0:T(128)} %param.15) | copy-start | bytes 1540
  122.0 110.7 %copy-start.1 = (bf16[128,512]{1,0:T(8,128)(2,1)S(1)}, bf16[128,512]{1,0:T(8,128)(2,1)}, u32[]{:S(2)}) copy-start(bf16[128,512]{1,0:T(8,128)(2,1)} %param.13) | copy-start | bytes 393220
  122.0 76.4 %reduce-scatter.10.cloned.1.call-start = ((), (), s32[]{:S(2)}) async-start(), calls=%async_computation.8 | async-start | bytes 655360 | tf_op jit(solution)/shard_map/reduce_scatter | solution.py:30
  178.7 151.3 %reduce-scatter.12.cloned.1.call-start = ((), (), s32[]{:S(2)}) async-start(), calls=%async_computation.9 | async-start | bytes 3899392 | tf_op jit(solution)/shard_map/reduce_scatter | solution.py:79
  249.0 150.9 %all-gather.4.cloned.1.call-start = ((), (), s32[]{:S(2)}) async-start(), calls=%async_computation.10 | async-start | bytes 7798784 | tf_op jit(solution)/shard_map/all_gather | solution.py:26
  332.0 89.7 %reduce-scatter.18.cloned.1.call-start = ((), (), s32[]{:S(2)}) async-start(), calls=%async_computation.13 | async-start | bytes 5505024 | tf_op jit(solution)/shard_map/reduce_scatter | solution.py:108
  338.1 102.4 %reduce-scatter.20.cloned.1.call-start = ((), (), s32[]{:S(2)}) async-start(), calls=%async_computation.14 | async-start | bytes 655360 | tf_op jit(solution)/shard_map/reduce_scatter | solution.py:30
  399.9 5.4 %copy-start.5 = (bf16[2,512,3584]{2,1,0:T(8,128)(2,1)S(1)}, bf16[2,512,3584]{2,1,0:T(8,128)(2,1)}, u32[]{:S(2)}) copy-start(bf16[2,512,3584]{2,1,0:T(8,128)(2,1)} %all-gather.4.cloned.1.call-done) | copy-start | bytes 22020100
  399.9 6.3 %copy-start.7 = (bf16[512,3584]{1,0:T(8,128)(2,1)S(1)}, bf16[512,3584]{1,0:T(8,128)(2,1)}, u32[]{:S(2)}) copy-start(bf16[512,3584]{1,0:T(8,128)(2,1)} %param.10) | copy-start | bytes 11010052
  409.1 50.3 %reduce-scatter.16.cloned.1.call-start = ((), (), s32[]{:S(2)}) async-start(), calls=%async_computation.12 | async-start | bytes 5505024 | tf_op jit(solution)/shard_map/reduce_scatter | solution.py:102
  415.3 62.7 %reduce-scatter.14.cloned.1.call-start = ((), (), s32[]{:S(2)}) async-start(), calls=%async_computation.11 | async-start | bytes 5505024 | tf_op jit(solution)/shard_map/reduce_scatter | solution.py:96
Sparse Core Ops, SparseCore 0:
  35.1 84.8 reduce-scatter.7
  122.9 49.6 all-gather.5
  178.8 19.5 reduce-scatter.9
  249.1 80.8 reduce-scatter.11
  332.8 67.0 all-gather.3
  402.8 14.3 reduce-scatter.17
  419.6 20.8 reduce-scatter.19
  443.4 15.8 reduce-scatter.15
  462.4 15.5 reduce-scatter.13
where the time goes:
time: 489 us; the launch traced here: 488 us
  waiting for transfers between devices  345 us (71%)
  blocking collectives  56.9 us (12%)
  matrix products  47.8 us (10%)
  other arithmetic  15.5 us (3%)
  between operations  14 us (3%)
  local copies, waits for them, and re-layouts  8.87 us (2%)
    all_gather x2, waiting for transfers between devices, gather_hidden(): return lax.all_gather(stacked, 'row', axis=1, tiled=True)  112 us
    reduce_scatter x1, waiting for transfers between devices, per_device(): lax.psum_scatter(jnp.concatenate([jnp.dot(rows, gate_weight, preferred_el...  84.9 us
    reduce_scatter x1, waiting for transfers between devices, per_device(): lax.psum_scatter(right_transpose(rows, down_weight).astype(jnp.bfloat16),...  81 us
    reduce_scatter x2, waiting for transfers between devices, column_total(): lax.psum_scatter(term_fn(jnp.int32(0), count_rows * lax.axis_size('col'))...  34.6 us
    psum x1, blocking collectives, per_device(): score = lax.psum(partial_score, 'row')  33.2 us
    all_gather x2, blocking collectives, gather_tokens(): return lax.all_gather(block, 'col', axis=0, tiled=True)  23.8 us
    dot_general x3, matrix products, transpose_product(): lax.dot_general(left, right, (((0,), (0,)), ((), ())), preferred_element_...  18.2 us
    reduce_scatter x1, waiting for transfers between devices, per_device(): lax.psum_scatter(transpose_product(gathered, grads_all[1]).astype(jnp.bfl...  17.1 us
  transfers between devices with their start and end apart: 9, of which 8 were waited for; matrix products, arithmetic and copies ran while one was open for 7% of the time, Pallas kernels for 0%

commit v1 on v0

--- a/solution.py
+++ b/solution.py
@@ -4,6 +4,12 @@
 from jax.sharding import PartitionSpec as P
 
 reward_weight = 8.0
+
+
+def gather_and_add(block, name):
+    parts = lax.all_gather(block, name, axis=0, tiled=False)
+    total = parts.sum(axis=0)
+    return total
 
 
 def transpose_product(left, right):
@@ -66,7 +72,7 @@
     outcome = inputs.astype(jnp.float32) + mixed
     head_value = reward_head.astype(jnp.float32)
     partial_score = jnp.dot(outcome, head_value, precision=lax.Precision.HIGHEST)
-    score = lax.psum(partial_score, "row")
+    score = gather_and_add(partial_score, "row")
     slope = (
         reward_weight
         * label_mask.astype(jnp.float32)

time: 489 us -> 473 us (0.967)
  blocking collectives: 56.9 us -> 39.8 us
    psum x1 -> x0, blocking collectives: 33.2 us -> none  [per_device(): score = lax.psum(partial_score, 'row')]
    all_gather x0 -> x1, blocking collectives: none -> 16.3 us  [gather_and_add(): parts = lax.all_gather(block, name, axis=0, tiled=False)]
  transfers between devices with their start and end apart: 9 -> 9, of which waited for: 8 -> 8; matrix products, arithmetic and copies ran while one was open for 7% -> 8% of each run, Pallas kernels for 0% -> 0%
where the time goes in v1:
time: 473 us; the launch traced here: 472 us
  waiting for transfers between devices  345 us (73%)
  matrix products  47.8 us (10%)
  blocking collectives  39.8 us (8%)
  other arithmetic  15.5 us (3%)
  between operations  14 us (3%)
  local copies, waits for them, and re-layouts  8.87 us (2%)
    all_gather x2, waiting for transfers between devices, gather_hidden(): return lax.all_gather(stacked, 'row', axis=1, tiled=True)  112 us
    reduce_scatter x1, waiting for transfers between devices, per_device(): lax.psum_scatter(jnp.concatenate([jnp.dot(rows, gate_weight, preferred_el...  84.9 us
    reduce_scatter x1, waiting for transfers between devices, per_device(): lax.psum_scatter(right_transpose(rows, down_weight).astype(jnp.bfloat16),...  81.6 us
    reduce_scatter x2, waiting for transfers between devices, column_total(): lax.psum_scatter(term_fn(jnp.int32(0), count_rows * lax.axis_size('col'))...  34.6 us
    all_gather x2, blocking collectives, gather_tokens(): return lax.all_gather(block, 'col', axis=0, tiled=True)  23.5 us
    dot_general x3, matrix products, transpose_product(): lax.dot_general(left, right, (((0,), (0,)), ((), ())), preferred_element_...  18.3 us
    reduce_scatter x1, waiting for transfers between devices, per_device(): lax.psum_scatter(transpose_product(gathered, grads_all[1]).astype(jnp.bfl...  17.1 us
    all_gather x1, blocking collectives, gather_and_add(): parts = lax.all_gather(block, name, axis=0, tiled=False)  16.3 us
  transfers between devices with their start and end apart: 9, of which 8 were waited for; matrix products, arithmetic and copies ran while one was open for 8% of the time, Pallas kernels for 0%

profile of v1, /device:TPU:1, one launch (start us, length us, event | category | flops | bytes accessed | tf_op | source)
XLA Modules:
  0.0 472.0 jit_solution(14559898675121205872)
XLA Ops:
  7.2 0.0 reduce-scatter.8.cloned.1.call-start
  7.2 13.6 %all_gather.18 = bf16[512,512]{1,0:T(8,128)(2,1)S(1)} all-gather(bf16[128,512]{1,0:T(8,128)(2,1)} %param.8), channel_id=1, replica_groups=mesh['row'=16,'col'=4,'dp'=2] {'col'}, dimensions={0}, use_global_device_ids=true | all-gather | bytes 655360 | tf_op jit(solution)/shard_map/all_gather | solution.py:28
  20.8 0.0 copy-start.6
  20.8 4.3 convolution_convert_fusion.4
  25.1 0.0 copy-done.6
  25.1 3.9 convolution_convert_fusion.5
  29.0 6.0 %pad_maximum_fusion = bf16[512,7168]{1,0:T(8,128)(2,1)} fusion(bf16[512,3584]{1,0:T(8,128)(2,1)S(1)} %convolution_convert_fusion.4, bf16[512,3584]{1,0:T(8,128)(2,1)} %convolution_convert_fusion.5), kind=kLoop, calls=%fused_computation | loop fusion | flops 14680064 | bytes 14680064 | tf_op jit(solution)/shard_map/concatenate | solution.py:51
  35.0 0.0 reduce-scatter.8.cloned.1.call-update
  35.0 0.0 all-gather.8.cloned.1.call-start
  35.1 84.9 %reduce-scatter.8.cloned.1.call-done = bf16[32,7168]{1,0:T(8,128)(2,1)} async-done(((bf16[512,7168]{1,0:T(8,128)(2,1)}), bf16[32,7168]{1,0:T(8,128)(2,1)}) %reduce-scatter.8.cloned.1.call-update) | async-done | bytes 458768 | tf_op jit(solution)/shard_map/reduce_scatter | solution.py:50
  120.0 1.1 convert_element_type.76
  121.1 0.8 multiply_convert_fusion
  121.9 0.0 all-gather.8.cloned.1.call-update
  121.9 0.0 copy-start.2
  121.9 0.0 copy-start
  122.0 0.0 copy-start.3
  122.0 0.0 copy-start.4
  122.0 0.0 copy-start.1
  122.0 0.0 reduce-scatter.10.cloned.1.call-start
  122.0 50.6 %all-gather.8.cloned.1.call-done = bf16[512,3584]{1,0:T(8,128)(2,1)} async-done(((bf16[32,3584]{1,0:T(8,128)(2,1)}), bf16[512,3584]{1,0:T(8,128)(2,1)}) %all-gather.8.cloned.1.call-update) | async-done | bytes 3670032 | tf_op jit(solution)/shard_map/all_gather | solution.py:32
  172.7 6.0 %convolution_convert_fusion.6 = bf16[512,512]{1,0:T(8,128)(2,1)} fusion(bf16[512,3584]{1,0:T(8,128)(2,1)} %all-gather.8.cloned.1.call-done, bf16[3584,512]{1,0:T(8,128)(2,1)} %param.11), kind=kOutput, calls=%fused_computation.15 | convolution fusion | flops 1879310336 | bytes 7864320 | tf_op jit(solution)/shard_map/dot_general | solution.py:69
  178.7 0.0 reduce-scatter.10.cloned.1.call-update
  178.7 0.0 reduce-scatter.12.cloned.1.call-start
  178.7 0.0 copy-done.2
  178.8 19.6 %reduce-scatter.10.cloned.1.call-done = bf16[128,512]{1,0:T(8,128)(2,1)} async-done(((bf16[512,512]{1,0:T(8,128)(2,1)}), bf16[128,512]{1,0:T(8,128)(2,1)}) %reduce-scatter.10.cloned.1.call-update) | async-done | bytes 131088 | tf_op jit(solution)/shard_map/reduce_scatter | solution.py:36
  198.4 0.0 copy-done
  198.4 1.1 convolution_bitcast_fusion
  199.5 16.3 %all-gather.2 = f32[16,1,128]{2,1,0:T(1,128)S(1)} all-gather(f32[1,1,128]{2,1,0:T(1,128)S(1)} %convolution_bitcast_fusion), channel_id=3, replica_groups=mesh['row'=16,'col'=4,'dp'=2] {'row'}, dimensions={0}, use_global_device_ids=true | all-gather | bytes 8704 | tf_op jit(solution)/shard_map/all_gather | solution.py:10
  215.9 0.0 copy-done.3
  215.9 0.0 copy-done.4
  215.9 0.0 copy-done.1
  215.9 0.1 fusion.14
  216.0 9.9 %all_gather.22 = bf16[512,512]{1,0:T(8,128)(2,1)S(1)} all-gather(bf16[128,512]{1,0:T(8,128)(2,1)S(1)} %fusion.14), channel_id=1, replica_groups=mesh['row'=16,'col'=4,'dp'=2] {'col'}, dimensions={0}, use_global_device_ids=true | all-gather | bytes 655360 | tf_op jit(solution)/shard_map/all_gather | solution.py:28
  225.9 6.0 %convolution_convert_fusion.3 = bf16[512,3584]{1,0:T(8,128)(2,1)} fusion(bf16[512,512]{1,0:T(8,128)(2,1)S(1)} %all_gather.22, bf16[3584,512]{1,0:T(8,128)(2,1)} %param.11), kind=kOutput, calls=%fused_computation.4 | convolution fusion | flops 1880883200 | bytes 7864320 | tf_op jit(solution)/shard_map/dot_general | solution.py:22
  231.9 0.0 reduce-scatter.12.cloned.1.call-update
  231.9 0.0 all-gather.6.cloned.1.call-start
  232.0 81.6 %reduce-scatter.12.cloned.1.call-done = bf16[32,3584]{1,0:T(8,128)(2,1)} async-done(((bf16[512,3584]{1,0:T(8,128)(2,1)}), bf16[32,3584]{1,0:T(8,128)(2,1)}) %reduce-scatter.12.cloned.1.call-update) | async-done | bytes 229392 | tf_op jit(solution)/shard_map/reduce_scatter | solution.py:85
  313.5 1.2 fusion.16
  314.7 0.8 pad_maximum_fusion.1
  315.5 0.0 all-gather.6.cloned.1.call-update
  315.5 0.0 reduce-scatter.18.cloned.1.call-start
  315.6 6.0 %convolution_convert_fusion = bf16[3584,512]{1,0:T(8,128)(2,1)} fusion(bf16[512,3584]{1,0:T(8,128)(2,1)} %all-gather.8.cloned.1.call-done, bf16[512,512]{1,0:T(8,128)(2,1)S(1)} %all_gather.22), kind=kOutput, calls=%fused_computation.1 | convolution fusion | flops 1880883200 | bytes 7864320 | tf_op jit(solution)/shard_map/dot_general | solution.py:16
  321.6 0.0 reduce-scatter.18.cloned.1.call-update
  321.6 0.0 reduce-scatter.20.cloned.1.call-start
  321.6 61.8 %all-gather.6.cloned.1.call-done = bf16[2,512,3584]{2,1,0:T(8,128)(2,1)} async-done(((bf16[2,32,3584]{2,1,0:T(8,128)(2,1)}), bf16[2,512,3584]{2,1,0:T(8,128)(2,1)}) %all-gather.6.cloned.1.call-update) | async-done | bytes 7340048 | tf_op jit(solution)/shard_map/all_gather | solution.py:32
  383.4 5.4 %fusion.2 = f32[512,512]{1,0:T(8,128)S(1)} fusion(bf16[512,3584]{1,0:T(8,128)(2,1)} %param.9, bf16[2,512,3584]{2,1,0:T(8,128)(2,1)} %all-gather.6.cloned.1.call-done), kind=kOutput, calls=%fused_computation.11 | convolution fusion | flops 1879048192 | bytes 8388608 | tf_op jit(solution)/shard_map/dot_general | solution.py:22
  388.8 0.0 copy-done.5
  388.8 0.9 copy-done.7
  389.7 2.9 fusion.5
  392.6 0.0 reduce-scatter.20.cloned.1.call-update
  392.6 0.2 reduce-scatter.16.cloned.1.call-start
  392.8 6.0 %fusion.1 = bf16[512,3584]{0,1:T(8,128)(2,1)} fusion(bf16[512,512]{1,0:T(8,128)(2,1)S(1)} %all_gather.18, bf16[2,512,3584]{2,1,0:T(8,128)(2,1)} %all-gather.6.cloned.1.call-done), kind=kOutput, calls=%fused_computation.8 | convolution fusion | flops 1880883200 | bytes 7864320 | tf_op jit(solution)/shard_map/dot_general | solution.py:16
  398.8 0.0 reduce-scatter.16.cloned.1.call-update
  398.8 0.0 reduce-scatter.14.cloned.1.call-start
  398.9 6.3 %fusion = bf16[512,3584]{0,1:T(8,128)(2,1)} fusion(bf16[512,512]{1,0:T(8,128)(2,1)S(1)} %all_gather.18, bf16[2,512,3584]{2,1,0:T(8,128)(2,1)} %all-gather.6.cloned.1.call-done), kind=kOutput, calls=%fused_computation.7 | convolution fusion | flops 1880883200 | bytes 7864320 | tf_op jit(solution)/shard_map/dot_general | solution.py:16
  405.2 0.0 reduce-scatter.14.cloned.1.call-update
  405.2 0.0 reduce-scatter.18.cloned.1.call-done
  405.2 3.9 convert_element_type.94
  409.1 14.9 %reduce-scatter.20.cloned.1.call-done = bf16[128,512]{1,0:T(8,128)(2,1)} async-done(((bf16[512,512]{1,0:T(8,128)(2,1)}), bf16[128,512]{1,0:T(8,128)(2,1)}) %reduce-scatter.20.cloned.1.call-update) | async-done | bytes 131088 | tf_op jit(solution)/shard_map/reduce_scatter | solution.py:36
  424.0 1.7 convert_add_fusion
  425.7 17.1 %reduce-scatter.16.cloned.1.call-done = bf16[256,3584]{0,1:T(8,128)(2,1)} async-done(((bf16[512,3584]{0,1:T(8,128)(2,1)}), bf16[256,3584]{0,1:T(8,128)(2,1)}) %reduce-scatter.16.cloned.1.call-update) | async-done | bytes 1835024 | tf_op jit(solution)/shard_map/reduce_scatter | solution.py:108
  442.9 4.0 copy.15
  446.8 14.7 %reduce-scatter.14.cloned.1.call-done = bf16[256,3584]{0,1:T(8,128)(2,1)} async-done(((bf16[512,3584]{0,1:T(8,128)(2,1)}), bf16[256,3584]{0,1:T(8,128)(2,1)}) %reduce-scatter.14.cloned.1.call-update) | async-done | bytes 1835024 | tf_op jit(solution)/shard_map/reduce_scatter | solution.py:102
  461.5 4.0 copy.14
  (6 shorter events, 0.1 us)
Async XLA Ops:
  7.2 112.8 %reduce-scatter.8.cloned.1.call-start = ((), (), s32[]{:S(2)}) async-start(), calls=%async_computation.7 | async-start | bytes 7798784 | tf_op jit(solution)/shard_map/reduce_scatter | solution.py:50
  20.8 4.3 copy-start.6
  35.0 137.6 %all-gather.8.cloned.1.call-start = ((), (), s32[]{:S(2)}) async-start(), calls=%async_computation.15 | async-start | bytes 3899392 | tf_op jit(solution)/shard_map/all_gather | solution.py:32
  121.9 56.8 %copy-start.2 = (bf16[512]{0:T(512)(128)(2,1)S(1)}, bf16[512]{0:T(512)(128)(2,1)}, u32[]{:S(2)}) copy-start(bf16[512]{0:T(512)(128)(2,1)} %param.12) | copy-start | bytes 3076
  121.9 76.5 %copy-start = (bf16[128,512]{1,0:T(8,128)(2,1)S(1)}, bf16[128,512]{1,0:T(8,128)(2,1)}, u32[]{:S(2)}) copy-start(bf16[128,512]{1,0:T(8,128)(2,1)} %param.8) | copy-start | bytes 393220
  122.0 93.9 %copy-start.3 = (s32[128]{0:T(128)S(1)}, s32[128]{0:T(128)}, u32[]{:S(2)}) copy-start(s32[128]{0:T(128)} %param.14) | copy-start | bytes 1540
  122.0 93.9 %copy-start.4 = (s32[128]{0:T(128)S(1)}, s32[128]{0:T(128)}, u32[]{:S(2)}) copy-start(s32[128]{0:T(128)} %param.15) | copy-start | bytes 1540
  122.0 93.9 %copy-start.1 = (bf16[128,512]{1,0:T(8,128)(2,1)S(1)}, bf16[128,512]{1,0:T(8,128)(2,1)}, u32[]{:S(2)}) copy-start(bf16[128,512]{1,0:T(8,128)(2,1)} %param.13) | copy-start | bytes 393220
  122.0 76.4 %reduce-scatter.10.cloned.1.call-start = ((), (), s32[]{:S(2)}) async-start(), calls=%async_computation.8 | async-start | bytes 655360 | tf_op jit(solution)/shard_map/reduce_scatter | solution.py:36
  178.7 134.8 %reduce-scatter.12.cloned.1.call-start = ((), (), s32[]{:S(2)}) async-start(), calls=%async_computation.9 | async-start | bytes 3899392 | tf_op jit(solution)/shard_map/reduce_scatter | solution.py:85
  231.9 151.5 %all-gather.6.cloned.1.call-start = ((), (), s32[]{:S(2)}) async-start(), calls=%async_computation.10 | async-start | bytes 7798784 | tf_op jit(solution)/shard_map/all_gather | solution.py:32
  315.5 89.7 %reduce-scatter.18.cloned.1.call-start = ((), (), s32[]{:S(2)}) async-start(), calls=%async_computation.13 | async-start | bytes 5505024 | tf_op jit(solution)/shard_map/reduce_scatter | solution.py:114
  321.6 102.4 %reduce-scatter.20.cloned.1.call-start = ((), (), s32[]{:S(2)}) async-start(), calls=%async_computation.14 | async-start | bytes 655360 | tf_op jit(solution)/shard_map/reduce_scatter | solution.py:36
  383.4 5.4 %copy-start.5 = (bf16[2,512,3584]{2,1,0:T(8,128)(2,1)S(1)}, bf16[2,512,3584]{2,1,0:T(8,128)(2,1)}, u32[]{:S(2)}) copy-start(bf16[2,512,3584]{2,1,0:T(8,128)(2,1)} %all-gather.6.cloned.1.call-done) | copy-start | bytes 22020100
  383.4 6.3 %copy-start.7 = (bf16[512,3584]{1,0:T(8,128)(2,1)S(1)}, bf16[512,3584]{1,0:T(8,128)(2,1)}, u32[]{:S(2)}) copy-start(bf16[512,3584]{1,0:T(8,128)(2,1)} %param.10) | copy-start | bytes 11010052
  392.6 50.3 %reduce-scatter.16.cloned.1.call-start = ((), (), s32[]{:S(2)}) async-start(), calls=%async_computation.12 | async-start | bytes 5505024 | tf_op jit(solution)/shard_map/reduce_scatter | solution.py:108
  398.8 62.7 %reduce-scatter.14.cloned.1.call-start = ((), (), s32[]{:S(2)}) async-start(), calls=%async_computation.11 | async-start | bytes 5505024 | tf_op jit(solution)/shard_map/reduce_scatter | solution.py:102
Sparse Core Ops, SparseCore 0:
  35.1 84.8 reduce-scatter.7
  122.9 49.6 all-gather.7
  178.8 19.5 reduce-scatter.9
  232.0 81.4 reduce-scatter.11
  316.3 67.0 all-gather.5
  386.3 14.3 reduce-scatter.17
  403.1 20.8 reduce-scatter.19
  426.9 15.8 reduce-scatter.15
  445.9 15.5 reduce-scatter.13
